TPU v7x, 32 devices: a whole 2x2x4 slice. The times are simulated.
32 devices in a mesh: dp: 2 (over y), seq: 16 (over z, x, core).
Axes of the slice: x: 2, y: 2, z: 4, core: 2. Of those that a mesh axis runs over, the one named last changes fastest.
Arguments:
- tokens: bfloat16 [2, 8192, 1024], P('dp', 'seq'), may hold values from -50 to 50
- w_query: bfloat16 [1024, 1024], P(None, 'dp'), may hold values from -0.1875 to 0.1875
- w_key: bfloat16 [1024, 1024], P(None, 'dp'), may hold values from -0.1875 to 0.1875
- w_value: bfloat16 [1024, 1024], P(None, 'dp'), may hold values from -0.1875 to 0.1875
- w_out: bfloat16 [1024, 1024], P('dp'), may hold values from -0.1875 to 0.1875
- norm_gain: float32 [1024], replicated, may hold values from 0.1 to 1.9
Outputs:
- layer_out: bfloat16 [2, 8192, 1024], P('dp', 'seq')
All inputs are finite; a program needn't handle non-finite values.
Results may differ from a plain program's by a relative error of at most 0.017.
Values may be sent and summed in bfloat16 or wider, within the bound.
A program may use at most 128 MiB of HBM per device.

v0:
```python
import functools

import jax
import jax.numpy as jnp
from jax import lax
from jax.experimental import pallas as pl
from jax.experimental.pallas import tpu as pltpu
from jax.sharding import PartitionSpec as P

H = 8
DH = 128
GROUP = 8
DIRECT = ((3, 1),)
MESH = pl.DeviceIdType.MESH
F32 = jnp.float32
BF16 = jnp.bfloat16


class Scan:
    def __init__(self, seq, steps, state, total, before, send, recv, prior, fin, send_sem, recv_sem):
        self.seq, self.steps = seq, steps
        self.state, self.total, self.before = state, total, before
        self.send, self.recv, self.prior, self.fin = send, recv, prior, fin
        self.send_sem, self.recv_sem = send_sem, recv_sem
        self.half = state.shape[0] // 2
        self.core = lax.rem(seq, 2)
        self.mine = pl.ds(pl.multiple_of(self.core * self.half, 16), self.half)
        self.other = pl.ds(pl.multiple_of((1 - self.core) * self.half, 16), self.half)
        self.at = 0
        self.copies = []

    def bit(self, step):
        return lax.rem(self.seq // (1 << step), 2)

    def partner(self, step):
        return self.seq + (1 - 2 * self.bit(step)) * (1 << step)

    def push(self, src, dst, index, step):
        copy = pltpu.make_async_remote_copy(
            src_ref=src,
            dst_ref=dst,
            send_sem=self.send_sem.at[index],
            recv_sem=self.recv_sem.at[index],
            device_id={"seq": self.partner(step)},
            device_id_type=MESH,
        )
        copy.start()
        self.copies.append(copy)

    def begin(self):
        self.send[0] = self.state[self.other, :].astype(BF16)
        self.push(self.send.at[0], self.recv.at[0], 0, 0)

    def advance(self):
        step = self.at
        if step > self.steps:
            return
        self.at += 1
        self.copies[step].wait_recv()
        if step == self.steps:
            return
        came = self.recv[step].astype(F32)
        if step == 0:
            self.total[...] = self.state[self.mine, :] + came
            self.before[...] = jnp.zeros(self.before.shape, F32)
        else:
            self.before[...] += jnp.where(self.bit(step) == 1, came, 0.0)
            if step < self.steps - 1:
                self.total[...] += came
        if step < self.steps - 1:
            self.send[step + 1] = self.total[...].astype(BF16)
            self.push(self.send.at[step + 1], self.recv.at[step + 1], step + 1, step + 1)
        else:
            before = self.before[...]
            first = self.recv[0].astype(F32)
            extra = jnp.where(self.core == 0, self.state[self.mine, :], 0.0)
            self.fin[...] = (before + extra).astype(BF16)
            self.push(self.fin, self.prior.at[self.mine, :], self.steps, 0)
            self.prior[self.mine, :] = (before + jnp.where(self.core == 1, first, 0.0)).astype(BF16)

    def drain(self):
        while self.at <= self.steps:
            self.advance()

    def close(self):
        for copy in self.copies:
            copy.wait_send()


def kernel(
    n, steps, sub,
    tok_hbm, wq_hbm, wk_hbm, wv_hbm, wo_hbm, gain_ref, out_ref,
    tok, own, own_o, wide, wide_o, kvq, within, normed, acc,
    state_a, total_a, before_a, send_a, recv_a, prior_a, fin_a,
    state_b, total_b, before_b, send_b, recv_b, prior_b, fin_b,
    load_sem, sends, recvs,
    as_send, as_recv, bs_send, bs_recv,
):
    dp, seq = lax.axis_index("dp"), lax.axis_index("seq")
    length, width = tok.shape
    cols = own.shape[2]
    heads = cols // DH
    sources = [wk_hbm, wv_hbm, wq_hbm, wo_hbm]
    rank = lax.rem(seq, GROUP)
    core = lax.rem(seq, 2)
    xbit = lax.rem(seq // 2, 2)
    core_mate = seq + 1 - 2 * core
    x_mate = seq + 2 * (1 - 2 * xbit)
    zbit = lax.rem(seq // 4, 2)
    z_mate = seq + 4 * (1 - 2 * zbit)
    x_rank = rank + 2 * (1 - 2 * xbit)
    z_rank = rank + 4 * (1 - 2 * zbit)
    g_rank = z_rank + 2 * (1 - 2 * xbit)
    lanes = ("y", "x", "z", "g", "c0", "c1", "c2", "c3")

    loads = [pltpu.make_async_copy(tok_hbm, tok, load_sem.at[4])]
    for kind in range(4):
        dst = own.at[kind] if kind < 3 else own_o
        loads.append(pltpu.make_async_copy(sources[kind], dst, load_sem.at[kind]))
    for copy in loads:
        copy.start()

    barrier = pltpu.get_barrier_semaphore()
    for slot in range(1, n):
        pl.semaphore_signal(barrier, inc=1, device_id={"dp": lax.rem(dp + slot, n)}, device_id_type=MESH)
    for step in range(steps):
        bit = lax.rem(seq // (1 << step), 2)
        mate = seq + (1 - 2 * bit) * (1 << step)
        pl.semaphore_signal(barrier, inc=1, device_id={"seq": mate}, device_id_type=MESH)
    pl.semaphore_wait(barrier, n - 1 + steps)

    def direct(kind, s):
        return (kind, s) in DIRECT

    def rows_of(kind, who, s):
        region = sources[kind].shape[0] // sub
        size = region // (2 if direct(kind, s) else GROUP)
        return pl.ds(pl.multiple_of(s * region + who * size, 16), size)

    def place(kind, slot, rows):
        if kind < 3:
            return wide.at[slot - 1, kind, rows, :]
        return wide_o.at[slot - 1, rows, :]

    pieces = [[(kind, slot, s) for s in range(sub) for slot in range(1, n)] for kind in range(4)]
    remote, sent = {}, []

    def push(src, dst, send, recv, target):
        copy = pltpu.make_async_remote_copy(
            src_ref=src, dst_ref=dst, send_sem=send, recv_sem=recv, device_id=target, device_id_type=MESH
        )
        copy.start()
        sent.append(copy)
        return copy

    for kind in range(4):
        for piece in pieces[kind]:
            _, slot, s = piece
            index = (0, kind, slot - 1, s)
            rows = rows_of(kind, core if direct(kind, s) else rank, s)
            remote["y", piece] = push(
                sources[kind].at[rows, :], place(kind, slot, rows), sends.at[index], recvs.at[index],
                {"dp": lax.rem(dp - slot + n, n)},
            )

    def forward(name, piece, who, target):
        kind, slot, s = piece
        here = place(kind, slot, rows_of(kind, who, s))
        index = (lanes.index(name), kind, slot - 1, s)
        remote[name, piece] = push(here, here, sends.at[index], recvs.at[index], target)

    def relay(piece):
        remote["y", piece].wait_recv()
        if direct(piece[0], piece[2]):
            forward("c0", piece, core, {"seq": core_mate})
            return
        forward("x", piece, rank, {"seq": x_mate})
        forward("z", piece, rank, {"seq": z_mate})
        forward("c0", piece, rank, {"seq": core_mate})

    def relay_again(piece):
        if direct(piece[0], piece[2]):
            return
        even = (piece[1] + piece[2]) % 2 == 1
        remote["x", piece].wait_recv()
        if even:
            forward("g", piece, x_rank, {"seq": z_mate})
        forward("c1", piece, x_rank, {"seq": core_mate})
        remote["z", piece].wait_recv()
        if not even:
            forward("g", piece, z_rank, {"seq": x_mate})
        forward("c2", piece, z_rank, {"seq": core_mate})

    def relay_last(piece):
        if direct(piece[0], piece[2]):
            return
        remote["g", piece].wait_recv()
        forward("c3", piece, g_rank, {"seq": core_mate})

    order = [piece for kind in range(4) for piece in pieces[kind]]
    half_of = len(pieces[0]) // 2 or 1
    cuts = [0]
    for kind in range(4):
        base = kind * len(pieces[0])
        cuts += [base + half_of, base + len(pieces[0])]
    acts = (relay, relay_again, relay_last)
    done = [0, 0, 0]

    def pump(*goals):
        goals = [cuts[goal] for goal in goals]
        while any(at < goal for at, goal in zip(done, goals)):
            todo = [i for i in range(3) if done[i] < goals[i] and (i == 0 or done[i] < done[i - 1])]
            pick = min(todo, key=lambda i: done[i] + 2 * half_of * i)
            acts[pick](order[done[pick]])
            done[pick] += 1

    def ready(kind):
        for piece in pieces[kind]:
            for name in ("c0",) if direct(kind, piece[2]) else ("c0", "c1", "c2", "c3"):
                remote[name, piece].wait_recv()

    chunk = min(256, cols)

    def project(kind, slot):
        source = own.at[kind] if slot == 0 else wide.at[slot - 1, kind]

        @pl.loop(0, cols // chunk)
        def _(i):
            at = pl.ds(pl.multiple_of(i * chunk, 128), chunk)
            kvq[kind, slot, :, at] = jnp.dot(tok[...], source[:, at], preferred_element_type=F32).astype(BF16)

    def states(slot, ref, base):
        @pl.loop(0, heads)
        def _(h):
            at = pl.ds(pl.multiple_of(h * DH, DH), DH)
            ref[pl.ds(pl.multiple_of(base + h * DH, DH), DH), :] = lax.dot_general(
                kvq[0, slot, :, at], kvq[1, slot, :, at], (((0,), (0,)), ((), ())), preferred_element_type=F32
            )

    half = length // 2

    def inner(slot):
        @pl.loop(0, heads)
        def _(h):
            at = pl.ds(pl.multiple_of(h * DH, DH), DH)
            for begin in (0, half):
                end = begin + half
                scores = lax.dot_general(
                    kvq[2, slot, begin:end, at], kvq[0, slot, :end, at], (((1,), (1,)), ((), ())),
                    preferred_element_type=F32,
                )
                row = begin + lax.broadcasted_iota(jnp.int32, (half, end), 0)
                col = lax.broadcasted_iota(jnp.int32, (half, end), 1)
                scores = jnp.where(col <= row, scores, 0.0).astype(BF16)
                within[slot, begin:end, at] = jnp.dot(
                    scores, kvq[1, slot, :end, at], preferred_element_type=F32
                )

    def finish(slot, prior, base):
        owner = lax.rem(dp + slot, n)

        @pl.loop(0, heads)
        def _(h):
            at = pl.ds(pl.multiple_of(h * DH, DH), DH)
            carried = jnp.dot(
                kvq[2, slot, :, at], prior[pl.ds(pl.multiple_of(base + h * DH, DH), DH), :],
                preferred_element_type=F32,
            )
            mixed = within[slot, :, at] + carried
            scale = lax.rsqrt(jnp.sum(mixed * mixed, axis=-1, keepdims=True) * (1.0 / DH) + 1e-05)
            normed[slot, :, at] = (mixed * scale * gain_ref[pl.ds(owner * heads + h, 1), :]).astype(BF16)

    def join(slot):
        source = own_o if slot == 0 else wide_o.at[slot - 1]

        @pl.loop(0, width // 256)
        def _(i):
            at = pl.ds(pl.multiple_of(i * 256, 128), 256)
            part = jnp.dot(normed[slot], source[:, at], preferred_element_type=F32)
            if slot > 0:
                part = acc[:, at] + part
            if slot == n - 1:
                out_ref[:, at] = part.astype(BF16)
            else:
                acc[:, at] = part

    scan_a = Scan(seq, steps, state_a, total_a, before_a, send_a, recv_a, prior_a, fin_a, as_send, as_recv)
    scan_b = Scan(seq, steps, state_b, total_b, before_b, send_b, recv_b, prior_b, fin_b, bs_send, bs_recv)

    others = range(1, n)
    loads[0].wait()
    loads[1].wait()
    project(0, 0)
    pump(1, 0, 0)
    loads[2].wait()
    project(1, 0)
    pump(2, 0, 0)
    states(0, state_a, 0)
    scan_a.begin()
    pump(3, 0, 0)
    loads[3].wait()
    project(2, 0)
    pump(4, 1, 0)
    scan_a.advance()
    inner(0)
    pump(5, 3, 1)
    scan_a.advance()
    pump(6, 4, 2)
    ready(0)
    for slot in others:
        project(0, slot)
    pump(7, 5, 3)
    scan_a.advance()
    pump(8, 6, 4)
    ready(1)
    for slot in others:
        project(1, slot)
        states(slot, state_b, (slot - 1) * cols)
    scan_b.begin()
    scan_a.advance()
    pump(8, 7, 5)
    scan_b.advance()
    scan_a.drain()
    finish(0, prior_a, 0)
    scan_b.advance()
    pump(8, 8, 6)
    loads[4].wait()
    join(0)
    scan_b.advance()
    ready(2)
    for slot in others:
        project(2, slot)
    pump(8, 8, 7)
    scan_b.advance()
    for slot in others:
        inner(slot)
    pump(8, 8, 8)
    scan_b.drain()
    for slot in others:
        finish(slot, prior_b, (slot - 1) * cols)
    ready(3)
    for slot in others:
        join(slot)
    for copy in sent:
        copy.wait_send()
    scan_a.close()
    scan_b.close()


def body(n, seqs, tokens, w_query, w_key, w_value, w_out, norm_gain):
    length, width = tokens.shape[1:]
    cols = w_query.shape[1]
    depth = w_out.shape[0]
    steps = seqs.bit_length() - 1
    sub = 2 if n <= 2 else 1
    any_spec = pl.BlockSpec(memory_space=pl.ANY)
    vmem = pl.BlockSpec(memory_space=pltpu.VMEM)
    scans = []
    for rows in (cols, (n - 1) * cols):
        part = rows // 2
        scans += [
            pltpu.VMEM((rows, DH), F32),
            pltpu.VMEM((part, DH), F32),
            pltpu.VMEM((part, DH), F32),
            pltpu.VMEM((steps, part, DH), BF16),
            pltpu.VMEM((steps, part, DH), BF16),
            pltpu.VMEM((rows, DH), BF16),
            pltpu.VMEM((part, DH), BF16),
        ]
    out = pl.pallas_call(
        functools.partial(kernel, n, steps, sub),
        out_shape=jax.ShapeDtypeStruct((length, width), BF16),
        in_specs=[any_spec] * 5 + [vmem],
        out_specs=vmem,
        scratch_shapes=[
            pltpu.VMEM((length, width), BF16),
            pltpu.VMEM((3, width, cols), BF16),
            pltpu.VMEM((depth, width), BF16),
            pltpu.VMEM((n - 1, 3, width, cols), BF16),
            pltpu.VMEM((n - 1, depth, width), BF16),
            pltpu.VMEM((3, n, length, cols), BF16),
            pltpu.VMEM((n, length, cols), F32),
            pltpu.VMEM((n, length, cols), BF16),
            pltpu.VMEM((length, width), F32),
        ]
        + scans
        + [pltpu.SemaphoreType.DMA((5,))]
        + [pltpu.SemaphoreType.DMA((8, 4, n - 1, sub))] * 2
        + [pltpu.SemaphoreType.DMA((steps + 1,))] * 4,
        compiler_params=pltpu.CompilerParams(
            collective_id=0, has_side_effects=True, vmem_limit_bytes=67043328
        ),
    )(tokens[0], w_query, w_key, w_value, w_out, norm_gain.reshape(-1, DH))
    return out[None]


def solution(mesh):
    in_specs = (
        P("dp", "seq", None),
        P(None, "dp"),
        P(None, "dp"),
        P(None, "dp"),
        P("dp", None),
        P(),
    )
    out_specs = P("dp", "seq", None)
    fn = functools.partial(body, mesh.shape["dp"], mesh.shape["seq"])
    return jax.shard_map(fn, mesh=mesh, in_specs=in_specs, out_specs=out_specs, check_vma=False)
```

profile of v0, /device:TPU:0, one launch (start us, length us, event | category | flops | bytes accessed | tf_op | source)
XLA Modules:
  0.0 47.5 jit_solution(14543722335343991412)
XLA Ops:
  0.0 45.3 %shard_map.64 = bf16[512,1024]{1,0:T(8,128)(2,1)} custom-call(bf16[512,1024]{1,0:T(8,128)(2,1)} %bitcast.4, bf16[1024,512]{1,0:T(8,128)(2,1)} %wq_hbm.1, bf16[1024,512]{1,0:T(8,128)(2,1)} %wk_hbm.1, bf16[1024,512]{1,0:T(8,128)(2,1)} %wv_hbm.1, bf16[512,1024]{1,0:T(8,128)(2,1)} %wo_hbm.1, f32[8,128]{1,0:T(8,128)} %bitcast.5), custom_call_target="tpu_custom_call" | custom-call | tf_op jit(solution)/shard_map/pallas_call | solution.py:370
  45.3 2.3 %copy.8 = bf16[1,512,1024]{2,1,0:T(8,128)(2,1)} copy(bf16[1,512,1024]{2,1,0:T(8,128)(2,1)} %bitcast.3) | data formatting | bytes 2097152
where the time goes:
time: 47.7 us; the launch traced here: 47.5 us
  Pallas kernels  45.3 us (95%)
  local copies, waits for them, and re-layouts  2.26 us (5%)
    pallas_call x1, Pallas kernels, body(): pl.pallas_call(functools.partial(kernel, n, steps, sub), out_shape=jax.Sh...  45.3 us
    unnamed x1, local copies, waits for them, and re-layouts  2.26 us

commit v1 on v0

v1 whole, which is shorter than its diff:
```python
import functools

import jax
import jax.numpy as jnp
from jax import lax
from jax.experimental import pallas as pl
from jax.experimental.pallas import tpu as pltpu
from jax.sharding import PartitionSpec as P

DH = 128
GROUP = 8
PLANE = 4
LAG = 3
DIRECT = ((1, 1, 1), (3, 1, 1))
MESH = pl.DeviceIdType.MESH
F32 = jnp.float32
BF16 = jnp.bfloat16


class Scan:
    def __init__(self, seq, outer, state, prior, out1, in1, total, in2, out3, sends, recvs):
        self.seq, self.outer = seq, outer
        self.state, self.prior = state, prior
        self.out1, self.in1, self.total, self.in2, self.out3 = out1, in1, total, in2, out3
        self.sends, self.recvs = sends, recvs
        self.share = state.shape[0] // PLANE
        self.me = lax.rem(seq, PLANE)
        self.row = seq // PLANE
        self.mine = self.rows(self.me)
        self.up, self.across, self.down = [], [], []

    def rows(self, owner):
        return pl.ds(pl.multiple_of(owner * self.share, 16), self.share)

    def copy(self, src, dst, index, target):
        return pltpu.make_async_remote_copy(
            src_ref=src,
            dst_ref=dst,
            send_sem=self.sends.at[index],
            recv_sem=self.recvs.at[index],
            device_id={"seq": target},
            device_id_type=MESH,
        )

    def plane(self, k):
        return lax.rem(self.me + k, PLANE)

    def begin(self):
        self.out1[...] = self.state[...].astype(BF16)
        for k in range(1, PLANE):
            target = self.plane(k)
            copy = self.copy(
                self.out1.at[self.rows(target), :], self.in1.at[k - 1], k - 1, self.seq - self.me + target
            )
            copy.start()
            self.up.append(copy)

    def middle(self):
        for copy in self.up:
            copy.wait_recv()
        total = self.state[self.mine, :]
        for k in range(1, PLANE):
            total = total + self.in1[k - 1].astype(F32)
        self.total[...] = total.astype(BF16)
        for k in range(1, self.outer):
            copy = self.copy(self.total, self.in2.at[k - 1], PLANE - 2 + k, self.seq + k * PLANE)
            pl.when(self.row + k < self.outer)(copy.start)
            self.across.append(copy)

    def last(self):
        before = jnp.zeros((self.share, DH), F32)
        for k in range(1, self.outer):
            pl.when(self.row >= k)(self.across[k - 1].wait_recv)
            before = before + jnp.where(self.row >= k, self.in2[k - 1].astype(F32), 0.0)
        parts = [(self.me, self.state[self.mine, :])]
        for k in range(1, PLANE):
            parts.append((self.plane(PLANE - k), self.in1[k - 1].astype(F32)))

        def prefix(target):
            result = before
            for source, part in parts:
                result = result + jnp.where(source < target, part, 0.0)
            return result.astype(BF16)

        for k in range(1, PLANE):
            target = self.plane(k)
            self.out3[k - 1] = prefix(target)
            copy = self.copy(
                self.out3.at[k - 1], self.prior.at[self.mine, :], PLANE - 3 + self.outer + k,
                self.seq - self.me + target,
            )
            copy.start()
            self.down.append(copy)
        self.prior[self.mine, :] = prefix(self.me)

    def end(self):
        for copy in self.down:
            copy.wait_recv()

    def close(self):
        for copy in self.up + self.down:
            copy.wait_send()
        for k in range(1, self.outer):
            pl.when(self.row + k < self.outer)(self.across[k - 1].wait_send)


def kernel(
    n, seqs, parts,
    tok_hbm, wq_hbm, wk_hbm, wv_hbm, wo_hbm, gain_ref, out_ref,
    tok, own, own_o, wide, wide_o, kvq, within, normed, acc,
    load_sem, sends, recvs, *scan_refs,
):
    dp, seq = lax.axis_index("dp"), lax.axis_index("seq")
    length, width = tok.shape
    cols = own.shape[2]
    pairs, lanes_per = wide.shape[2], wide.shape[4]
    outer = seqs // PLANE
    sources = [wk_hbm, wv_hbm, wq_hbm, wo_hbm]
    rank = lax.rem(seq, GROUP)
    core = lax.rem(seq, 2)
    xbit = lax.rem(seq // 2, 2)
    core_mate = seq + 1 - 2 * core
    x_mate = seq + 2 * (1 - 2 * xbit)
    zbit = lax.rem(seq // 4, 2)
    z_mate = seq + 4 * (1 - 2 * zbit)
    x_rank = rank + 2 * (1 - 2 * xbit)
    z_rank = rank + 4 * (1 - 2 * zbit)
    g_rank = z_rank + 2 * (1 - 2 * xbit)
    lanes = ("y", "x", "z", "g", "c0", "c1", "c2", "c3")

    loads = [pltpu.make_async_copy(tok_hbm, tok, load_sem.at[4])]
    for kind in range(4):
        dst = own.at[kind] if kind < 3 else own_o
        loads.append(pltpu.make_async_copy(sources[kind], dst, load_sem.at[kind]))
    for copy in loads:
        copy.start()

    barrier = pltpu.get_barrier_semaphore()
    for slot in range(1, n):
        pl.semaphore_signal(barrier, inc=1, device_id={"dp": lax.rem(dp + slot, n)}, device_id_type=MESH)
    for k in range(1, outer):
        pl.semaphore_signal(barrier, inc=1, device_id={"seq": lax.rem(seq + k * PLANE, seqs)}, device_id_type=MESH)
    place_in = lax.rem(seq, PLANE)
    for k in range(1, PLANE):
        mate = seq - place_in + lax.rem(place_in + k, PLANE)
        pl.semaphore_signal(barrier, inc=1, device_id={"seq": mate}, device_id_type=MESH)
    pl.semaphore_wait(barrier, n - 1 + outer - 1 + PLANE - 1)

    def direct(piece):
        return (piece[0], piece[2], piece[3]) in DIRECT

    def rows_of(piece, who):
        kind, _, p, s = piece
        region = (width if kind < 3 else lanes_per) // parts
        size = region // (2 if direct(piece) else GROUP)
        base = s * region + (p * lanes_per if kind == 3 else 0)
        return pl.ds(pl.multiple_of(base + who * size, 16), size)

    def place(piece, rows):
        kind, slot, p, _ = piece
        if kind < 3:
            return wide.at[slot - 1, kind, p, rows, :]
        return wide_o.at[slot - 1, rows, :]

    order, mark = [], {}
    for kinds in ((0, 1), (2,), (3,)):
        for p in range(pairs):
            for kind in kinds:
                order += [(kind, slot, p, s) for s in range(parts) for slot in range(1, n)]
                mark[kind, p] = len(order)
    remote, sent = {}, []

    def push(src, dst, index, target):
        copy = pltpu.make_async_remote_copy(
            src_ref=src, dst_ref=dst, send_sem=sends.at[index], recv_sem=recvs.at[index],
            device_id=target, device_id_type=MESH,
        )
        copy.start()
        sent.append(copy)
        return copy

    def index_of(name, piece):
        kind, slot, p, s = piece
        return (lanes.index(name), kind, slot - 1, p, s)

    for piece in order:
        kind, slot, p, _ = piece
        rows = rows_of(piece, core if direct(piece) else rank)
        if kind < 3:
            src = sources[kind].at[rows, pl.ds(p * lanes_per, lanes_per)]
        else:
            src = sources[kind].at[rows, :]
        remote["y", piece] = push(src, place(piece, rows), index_of("y", piece), {"dp": lax.rem(dp - slot + n, n)})

    def forward(name, piece, who, target):
        here = place(piece, rows_of(piece, who))
        remote[name, piece] = push(here, here, index_of(name, piece), {"seq": target})

    def relay(piece):
        remote["y", piece].wait_recv()
        if direct(piece):
            forward("c0", piece, core, core_mate)
            return
        forward("x", piece, rank, x_mate)
        forward("z", piece, rank, z_mate)
        forward("c0", piece, rank, core_mate)

    def relay_again(piece):
        if direct(piece):
            return
        even = (piece[1] + piece[3]) % 2 == 1
        remote["x", piece].wait_recv()
        if even:
            forward("g", piece, x_rank, z_mate)
        forward("c1", piece, x_rank, core_mate)
        remote["z", piece].wait_recv()
        if not even:
            forward("g", piece, z_rank, x_mate)
        forward("c2", piece, z_rank, core_mate)

    def relay_last(piece):
        if direct(piece):
            return
        remote["g", piece].wait_recv()
        forward("c3", piece, g_rank, core_mate)

    acts = (relay, relay_again, relay_last)
    done = [0, 0, 0]

    def go(*goals):
        goals = [max(at, goal * len(order) // 16) for at, goal in zip(done, goals)]
        goals[0] = max(goals)
        goals[1] = max(goals[1:])
        while any(at < goal for at, goal in zip(done, goals)):
            todo = [i for i in range(3) if done[i] < goals[i] and (i == 0 or done[i] < done[i - 1])]
            pick = min(todo, key=lambda i: done[i] + LAG * i)
            acts[pick](order[done[pick]])
            done[pick] += 1

    def ready(kind, p):
        assert done[2] >= mark[kind, p]
        for piece in order:
            if (piece[0], piece[2]) == (kind, p):
                for name in ("c0",) if direct(piece) else ("c0", "c1", "c2", "c3"):
                    remote[name, piece].wait_recv()

    def lane(i, size):
        return pl.ds(pl.multiple_of(i * size, 128), size)

    def project_own(kind):
        @pl.loop(0, pairs)
        def _(p):
            at = lane(p, lanes_per)
            kvq[kind, 0, :, at] = jnp.dot(tok[...], own[kind, :, at], preferred_element_type=F32).astype(BF16)

    def project(kind, p):
        for slot in range(1, n):
            at = pl.ds(p * lanes_per, lanes_per)
            kvq[kind, slot, :, at] = jnp.dot(
                tok[...], wide[slot - 1, kind, p], preferred_element_type=F32
            ).astype(BF16)

    per = lanes_per // DH

    def states(slot, first, count, ref, base):
        @pl.loop(0, count)
        def _(h):
            at = lane(first + h, DH)
            ref[pl.ds(pl.multiple_of(base + h * DH, DH), DH), :] = lax.dot_general(
                kvq[0, slot, :, at], kvq[1, slot, :, at], (((0,), (0,)), ((), ())), preferred_element_type=F32
            )

    half = length // 2

    def inner(slot, first, count):
        @pl.loop(0, count)
        def _(h):
            at = lane(first + h, DH)
            for begin in (0, half):
                end = begin + half
                scores = lax.dot_general(
                    kvq[2, slot, begin:end, at], kvq[0, slot, :end, at], (((1,), (1,)), ((), ())),
                    preferred_element_type=F32,
                )
                row = begin + lax.broadcasted_iota(jnp.int32, (half, end), 0)
                col = lax.broadcasted_iota(jnp.int32, (half, end), 1)
                scores = jnp.where(col <= row, scores, 0.0).astype(BF16)
                within[slot, begin:end, at] = jnp.dot(
                    scores, kvq[1, slot, :end, at], preferred_element_type=F32
                )

    heads = cols // DH

    def finish(slot, first, count, prior, base):
        owner = lax.rem(dp + slot, n)

        @pl.loop(0, count)
        def _(h):
            at = lane(first + h, DH)
            carried = jnp.dot(
                kvq[2, slot, :, at], prior[pl.ds(pl.multiple_of(base + h * DH, DH), DH), :],
                preferred_element_type=F32,
            )
            mixed = within[slot, :, at] + carried
            scale = lax.rsqrt(jnp.sum(mixed * mixed, axis=-1, keepdims=True) * (1.0 / DH) + 1e-05)
            gain = gain_ref[pl.ds(owner * heads + first + h, 1), :]
            normed[slot, :, at] = (mixed * scale * gain).astype(BF16)

    def join_own():
        @pl.loop(0, width // 256)
        def _(i):
            at = lane(i, 256)
            acc[:, at] = jnp.dot(normed[0], own_o[:, at], preferred_element_type=F32)

    def join(p):
        for slot in range(1, n):
            @pl.loop(0, width // 256)
            def _(i):
                at = lane(i, 256)
                span = pl.ds(p * lanes_per, lanes_per)
                part = acc[:, at] + jnp.dot(
                    normed[slot, :, span], wide_o[slot - 1, span, at], preferred_element_type=F32
                )
                if slot == n - 1 and p == pairs - 1:
                    out_ref[:, at] = part.astype(BF16)
                else:
                    acc[:, at] = part

    size = len(scan_refs) // (1 + pairs)
    scans = [Scan(seq, outer, *scan_refs[i * size:(i + 1) * size]) for i in range(1 + pairs)]
    scan_a, scan_b = scans[0], scans[1:]

    def states_b(p):
        for slot in range(1, n):
            states(slot, p * per, per, scan_b[p].state, (slot - 1) * lanes_per)
        scan_b[p].begin()

    def inner_b(p):
        for slot in range(1, n):
            inner(slot, p * per, per)

    def finish_b(p):
        scan_b[p].end()
        for slot in range(1, n):
            finish(slot, p * per, per, scan_b[p].prior, (slot - 1) * lanes_per)

    final = pairs - 1
    loads[0].wait()
    loads[1].wait()
    project_own(0)
    loads[2].wait()
    project_own(1)
    states(0, 0, heads, scan_a.state, 0)
    scan_a.begin()
    go(2, 0, 0)
    loads[3].wait()
    project_own(2)
    go(4, 1, 0)
    part = max(1, heads // 4)
    inner(0, 0, part)
    go(5, 2, 0)
    scan_a.middle()
    for i in range(1, heads // part):
        inner(0, i * part, part)
        go(5 + i, 2 + i, i - 1)
    scan_a.last()
    go(8, 6, 4)
    ready(0, 0)
    project(0, 0)
    if pairs == 1:
        go(8, 8, 8)
    ready(1, 0)
    project(1, 0)
    states_b(0)
    go(9, 7, 6)
    if pairs > 1:
        go(9, 8, 8)
        ready(0, final)
        project(0, final)
        ready(1, final)
        project(1, final)
        states_b(final)
    go(11, 9, 8)
    scan_b[0].middle()
    scan_a.end()
    finish(0, 0, heads, scan_a.prior, 0)
    go(13, 11, 9)
    if pairs > 1:
        scan_b[final].middle()
    loads[4].wait()
    join_own()
    go(15, 13, 11)
    scan_b[0].last()
    go(15, 14, 12)
    ready(2, 0)
    project(2, 0)
    inner_b(0)
    if pairs > 1:
        scan_b[final].last()
    go(15, 15, 13)
    if pairs > 1:
        ready(2, final)
        project(2, final)
        inner_b(final)
    finish_b(0)
    go(16, 16, 16)
    ready(3, 0)
    join(0)
    if pairs > 1:
        finish_b(final)
        ready(3, final)
        join(final)
    for copy in sent:
        copy.wait_send()
    for scan in scans:
        scan.close()


def body(n, seqs, tokens, w_query, w_key, w_value, w_out, norm_gain):
    length, width = tokens.shape[1:]
    cols = w_query.shape[1]
    depth = w_out.shape[0]
    lanes_per = min(256, cols)
    pairs = cols // lanes_per
    parts = 2 if n <= 2 else 1
    outer = seqs // PLANE
    any_spec = pl.BlockSpec(memory_space=pl.ANY)
    vmem = pl.BlockSpec(memory_space=pltpu.VMEM)
    scans = []
    for rows in [cols] + [(n - 1) * lanes_per] * pairs:
        share = rows // PLANE
        scans += [
            pltpu.VMEM((rows, DH), F32),
            pltpu.VMEM((rows, DH), BF16),
            pltpu.VMEM((rows, DH), BF16),
            pltpu.VMEM((PLANE - 1, share, DH), BF16),
            pltpu.VMEM((share, DH), BF16),
            pltpu.VMEM((outer - 1, share, DH), BF16),
            pltpu.VMEM((PLANE - 1, share, DH), BF16),
            pltpu.SemaphoreType.DMA((2 * (PLANE - 1) + outer - 1,)),
            pltpu.SemaphoreType.DMA((2 * (PLANE - 1) + outer - 1,)),
        ]
    out = pl.pallas_call(
        functools.partial(kernel, n, seqs, parts),
        out_shape=jax.ShapeDtypeStruct((length, width), BF16),
        in_specs=[any_spec] * 5 + [vmem],
        out_specs=vmem,
        scratch_shapes=[
            pltpu.VMEM((length, width), BF16),
            pltpu.VMEM((3, width, cols), BF16),
            pltpu.VMEM((depth, width), BF16),
            pltpu.VMEM((n - 1, 3, pairs, width, lanes_per), BF16),
            pltpu.VMEM((n - 1, depth, width), BF16),
            pltpu.VMEM((3, n, length, cols), BF16),
            pltpu.VMEM((n, length, cols), F32),
            pltpu.VMEM((n, length, cols), BF16),
            pltpu.VMEM((length, width), F32),
        ]
        + [pltpu.SemaphoreType.DMA((5,))]
        + [pltpu.SemaphoreType.DMA((8, 4, n - 1, pairs, parts))] * 2
        + scans,
        compiler_params=pltpu.CompilerParams(
            collective_id=0, has_side_effects=True, vmem_limit_bytes=67043328
        ),
    )(tokens[0], w_query, w_key, w_value, w_out, norm_gain.reshape(-1, DH))
    return out[None]


def solution(mesh):
    in_specs = (
        P("dp", "seq", None),
        P(None, "dp"),
        P(None, "dp"),
        P(None, "dp"),
        P("dp", None),
        P(),
    )
    out_specs = P("dp", "seq", None)
    fn = functools.partial(body, mesh.shape["dp"], mesh.shape["seq"])
    return jax.shard_map(fn, mesh=mesh, in_specs=in_specs, out_specs=out_specs, check_vma=False)
```

time: 47.7 us -> 51.3 us (1.075)
  Pallas kernels: 45.3 us -> 48.4 us
    pallas_call x1, Pallas kernels: 45.3 us -> 48.4 us  [body(): pl.pallas_call(functools.partial(kernel, n, seqs, parts), out_shape=jax.S...]
where the time goes in v1:
time: 51.3 us; the launch traced here: 50.6 us
  Pallas kernels  48.4 us (94%)
  local copies, waits for them, and re-layouts  2.26 us (4%)
    pallas_call x1, Pallas kernels, body(): pl.pallas_call(functools.partial(kernel, n, seqs, parts), out_shape=jax.S...  48.4 us
    unnamed x1, local copies, waits for them, and re-layouts  2.26 us

profile of v1, /device:TPU:0, one launch (start us, length us, event | category | flops | bytes accessed | tf_op | source)
XLA Modules:
  0.0 50.6 jit_solution(12242058279774790775)
XLA Ops:
  0.0 48.4 %shard_map.64 = bf16[512,1024]{1,0:T(8,128)(2,1)} custom-call(bf16[512,1024]{1,0:T(8,128)(2,1)} %bitcast.4, bf16[1024,512]{1,0:T(8,128)(2,1)} %wq_hbm.1, bf16[1024,512]{1,0:T(8,128)(2,1)} %wk_hbm.1, bf16[1024,512]{1,0:T(8,128)(2,1)} %wv_hbm.1, bf16[512,1024]{1,0:T(8,128)(2,1)} %wo_hbm.1, f32[8,128]{1,0:T(8,128)} %bitcast.5), custom_call_target="tpu_custom_call" | custom-call | tf_op jit(solution)/shard_map/pallas_call | solution.py:443
  48.4 2.3 %copy.8 = bf16[1,512,1024]{2,1,0:T(8,128)(2,1)} copy(bf16[1,512,1024]{2,1,0:T(8,128)(2,1)} %bitcast.3) | data formatting | bytes 2097152

commit v2 on v1

--- a/solution.py
+++ b/solution.py
@@ -10,8 +10,8 @@
 DH = 128
 GROUP = 8
 PLANE = 4
-LAG = 3
-DIRECT = ((1, 1, 1), (3, 1, 1))
+LAG = 4
+HALVES = {(0, 1): "x", (1, 1): "z"}
 MESH = pl.DeviceIdType.MESH
 F32 = jnp.float32
 BF16 = jnp.bfloat16
@@ -146,13 +146,21 @@
         pl.semaphore_signal(barrier, inc=1, device_id={"seq": mate}, device_id_type=MESH)
     pl.semaphore_wait(barrier, n - 1 + outer - 1 + PLANE - 1)
 
-    def direct(piece):
-        return (piece[0], piece[2], piece[3]) in DIRECT
+    def halves(piece):
+        return HALVES.get((piece[0], piece[2]))
+
+    def rank_of(piece):
+        axis = halves(piece)
+        return {"x": core + 2 * xbit, "z": core + 2 * zbit, None: rank}[axis]
+
+    def mate_of(piece):
+        axis = halves(piece)
+        return core + 2 * (1 - (xbit if axis == "x" else zbit))
 
     def rows_of(piece, who):
         kind, _, p, s = piece
         region = (width if kind < 3 else lanes_per) // parts
-        size = region // (2 if direct(piece) else GROUP)
+        size = region // (4 if halves(piece) else GROUP)
         base = s * region + (p * lanes_per if kind == 3 else 0)
         return pl.ds(pl.multiple_of(base + who * size, 16), size)
 
@@ -185,7 +193,7 @@
 
     for piece in order:
         kind, slot, p, _ = piece
-        rows = rows_of(piece, core if direct(piece) else rank)
+        rows = rows_of(piece, rank_of(piece))
         if kind < 3:
             src = sources[kind].at[rows, pl.ds(p * lanes_per, lanes_per)]
         else:
@@ -198,15 +206,18 @@
 
     def relay(piece):
         remote["y", piece].wait_recv()
-        if direct(piece):
-            forward("c0", piece, core, core_mate)
-            return
-        forward("x", piece, rank, x_mate)
-        forward("z", piece, rank, z_mate)
-        forward("c0", piece, rank, core_mate)
+        axis, who = halves(piece), rank_of(piece)
+        if axis != "z":
+            forward("x", piece, who, x_mate)
+        if axis != "x":
+            forward("z", piece, who, z_mate)
+        forward("c0", piece, who, core_mate)
 
     def relay_again(piece):
-        if direct(piece):
+        axis = halves(piece)
+        if axis:
+            remote[axis, piece].wait_recv()
+            forward("c1", piece, mate_of(piece), core_mate)
             return
         even = (piece[1] + piece[3]) % 2 == 1
         remote["x", piece].wait_recv()
@@ -219,7 +230,7 @@
         forward("c2", piece, z_rank, core_mate)
 
     def relay_last(piece):
-        if direct(piece):
+        if halves(piece):
             return
         remote["g", piece].wait_recv()
         forward("c3", piece, g_rank, core_mate)
@@ -238,10 +249,12 @@
             done[pick] += 1
 
     def ready(kind, p):
-        assert done[2] >= mark[kind, p]
+        if done[2] < mark[kind, p]:
+            top = -(-mark[kind, p] * 16 // len(order))
+            go(top, top, 0 if HALVES.get((kind, p)) else top)
         for piece in order:
             if (piece[0], piece[2]) == (kind, p):
-                for name in ("c0",) if direct(piece) else ("c0", "c1", "c2", "c3"):
+                for name in ("c0", "c1") if halves(piece) else ("c0", "c1", "c2", "c3"):
                     remote[name, piece].wait_recv()
 
     def lane(i, size):
@@ -345,6 +358,14 @@
             finish(slot, p * per, per, scan_b[p].prior, (slot - 1) * lanes_per)
 
     final = pairs - 1
+    part = max(1, heads // 4)
+    pieces = iter(range(heads // part))
+
+    def inner_next():
+        for i in pieces:
+            inner(0, i * part, part)
+            return
+
     loads[0].wait()
     loads[1].wait()
     project_own(0)
@@ -355,57 +376,58 @@
     go(2, 0, 0)
     loads[3].wait()
     project_own(2)
-    go(4, 1, 0)
-    part = max(1, heads // 4)
-    inner(0, 0, part)
+    go(4, 0, 0)
+    inner_next()
     go(5, 2, 0)
+    inner_next()
     scan_a.middle()
-    for i in range(1, heads // part):
-        inner(0, i * part, part)
-        go(5 + i, 2 + i, i - 1)
-    scan_a.last()
-    go(8, 6, 4)
+    go(6, 4, 0)
+    inner_next()
+    go(7, 4, 1)
+    inner_next()
+    go(8, 5, 3)
+    go(9, 5, 3)
     ready(0, 0)
     project(0, 0)
-    if pairs == 1:
-        go(8, 8, 8)
+    go(10, 6, 3)
+    scan_a.last()
+    go(12, 7, 4)
+    if pairs > 1:
+        ready(0, final)
+        project(0, final)
     ready(1, 0)
     project(1, 0)
     states_b(0)
-    go(9, 7, 6)
+    go(14, 9, 4)
     if pairs > 1:
-        go(9, 8, 8)
-        ready(0, final)
-        project(0, final)
         ready(1, final)
         project(1, final)
         states_b(final)
-    go(11, 9, 8)
-    scan_b[0].middle()
+    go(16, 10, 8)
     scan_a.end()
     finish(0, 0, heads, scan_a.prior, 0)
-    go(13, 11, 9)
+    go(16, 12, 9)
+    scan_b[0].middle()
+    loads[4].wait()
+    join_own()
+    go(16, 13, 10)
     if pairs > 1:
         scan_b[final].middle()
-    loads[4].wait()
-    join_own()
-    go(15, 13, 11)
-    scan_b[0].last()
-    go(15, 14, 12)
     ready(2, 0)
     project(2, 0)
     inner_b(0)
-    if pairs > 1:
-        scan_b[final].last()
-    go(15, 15, 13)
+    go(16, 15, 11)
+    scan_b[0].last()
     if pairs > 1:
         ready(2, final)
         project(2, final)
         inner_b(final)
+        scan_b[final].last()
+    go(16, 16, 14)
     finish_b(0)
-    go(16, 16, 16)
     ready(3, 0)
     join(0)
+    go(16, 16, 16)
     if pairs > 1:
         finish_b(final)
         ready(3, final)

time: 51.3 us -> 45.2 us (0.88)
  Pallas kernels: 48.4 us -> 42.6 us
    pallas_call x1, Pallas kernels: 48.4 us -> 42.6 us  [body(): pl.pallas_call(functools.partial(kernel, n, seqs, parts), out_shape=jax.S...]
where the time goes in v2:
time: 45.2 us; the launch traced here: 44.9 us
  Pallas kernels  42.6 us (94%)
  local copies, waits for them, and re-layouts  2.26 us (5%)
    pallas_call x1, Pallas kernels, body(): pl.pallas_call(functools.partial(kernel, n, seqs, parts), out_shape=jax.S...  42.6 us
    unnamed x1, local copies, waits for them, and re-layouts  2.26 us

profile of v2, /device:TPU:0, one launch (start us, length us, event | category | flops | bytes accessed | tf_op | source)
XLA Modules:
  0.0 44.9 jit_solution(15614793502929892962)
XLA Ops:
  0.0 42.6 %shard_map.64 = bf16[512,1024]{1,0:T(8,128)(2,1)} custom-call(bf16[512,1024]{1,0:T(8,128)(2,1)} %bitcast.4, bf16[1024,512]{1,0:T(8,128)(2,1)} %wq_hbm.1, bf16[1024,512]{1,0:T(8,128)(2,1)} %wk_hbm.1, bf16[1024,512]{1,0:T(8,128)(2,1)} %wv_hbm.1, bf16[512,1024]{1,0:T(8,128)(2,1)} %wo_hbm.1, f32[8,128]{1,0:T(8,128)} %bitcast.5), custom_call_target="tpu_custom_call" | custom-call | tf_op jit(solution)/shard_map/pallas_call | solution.py:465
  42.6 2.3 %copy.8 = bf16[1,512,1024]{2,1,0:T(8,128)(2,1)} copy(bf16[1,512,1024]{2,1,0:T(8,128)(2,1)} %bitcast.3) | data formatting | bytes 2097152

commit v3 on v2

--- a/solution.py
+++ b/solution.py
@@ -11,7 +11,7 @@
 GROUP = 8
 PLANE = 4
 LAG = 4
-HALVES = {(0, 1): "x", (1, 1): "z"}
+ROUTES = {(0, 1): "x", (1, 1): "z", (3, 0): "y", (3, 1): "y"}
 MESH = pl.DeviceIdType.MESH
 F32 = jnp.float32
 BF16 = jnp.bfloat16
@@ -106,9 +106,9 @@
 
 def kernel(
     n, seqs, parts,
-    tok_hbm, wq_hbm, wk_hbm, wv_hbm, wo_hbm, gain_ref, out_ref,
+    tok_hbm, wq_hbm, wk_hbm, wv_hbm, wo_hbm, gain_hbm, out_ref,
     tok, own, own_o, wide, wide_o, kvq, within, normed, acc,
-    load_sem, sends, recvs, *scan_refs,
+    gain_ref, load_sem, enter, sends, recvs, *scan_refs,
 ):
     dp, seq = lax.axis_index("dp"), lax.axis_index("seq")
     length, width = tok.shape
@@ -132,35 +132,46 @@
     for kind in range(4):
         dst = own.at[kind] if kind < 3 else own_o
         loads.append(pltpu.make_async_copy(sources[kind], dst, load_sem.at[kind]))
+    loads.append(pltpu.make_async_copy(gain_hbm, gain_ref, load_sem.at[5]))
     for copy in loads:
         copy.start()
 
     barrier = pltpu.get_barrier_semaphore()
     for slot in range(1, n):
         pl.semaphore_signal(barrier, inc=1, device_id={"dp": lax.rem(dp + slot, n)}, device_id_type=MESH)
-    for k in range(1, outer):
-        pl.semaphore_signal(barrier, inc=1, device_id={"seq": lax.rem(seq + k * PLANE, seqs)}, device_id_type=MESH)
+    row = seq // PLANE
+    above, below = row + 1 < outer, row >= 1
+
+    def tell(sem, target):
+        pl.semaphore_signal(sem, inc=1, device_id={"seq": target}, device_id_type=MESH)
+
+    pl.when(above)(lambda: tell(barrier, seq + PLANE))
+    pl.when(below)(lambda: tell(barrier, seq - PLANE))
     place_in = lax.rem(seq, PLANE)
     for k in range(1, PLANE):
         mate = seq - place_in + lax.rem(place_in + k, PLANE)
         pl.semaphore_signal(barrier, inc=1, device_id={"seq": mate}, device_id_type=MESH)
-    pl.semaphore_wait(barrier, n - 1 + outer - 1 + PLANE - 1)
-
-    def halves(piece):
-        return HALVES.get((piece[0], piece[2]))
+    pl.semaphore_wait(barrier, n - 1 + PLANE - 1 + above.astype(jnp.int32) + below.astype(jnp.int32))
+
+    def learn(k):
+        pl.when(below & (row + k - 1 < outer))(lambda: tell(enter, seq - PLANE))
+        pl.when(row + k < outer)(lambda: pl.semaphore_wait(enter, 1))
+
+    def route(piece):
+        return ROUTES.get((piece[0], piece[2]))
 
     def rank_of(piece):
-        axis = halves(piece)
-        return {"x": core + 2 * xbit, "z": core + 2 * zbit, None: rank}[axis]
+        axis = route(piece)
+        return {"x": core + 2 * xbit, "z": core + 2 * zbit, "y": core, None: rank}[axis]
 
     def mate_of(piece):
-        axis = halves(piece)
+        axis = route(piece)
         return core + 2 * (1 - (xbit if axis == "x" else zbit))
 
     def rows_of(piece, who):
         kind, _, p, s = piece
         region = (width if kind < 3 else lanes_per) // parts
-        size = region // (4 if halves(piece) else GROUP)
+        size = region // {"x": 4, "z": 4, "y": 2, None: GROUP}[route(piece)]
         base = s * region + (p * lanes_per if kind == 3 else 0)
         return pl.ds(pl.multiple_of(base + who * size, 16), size)
 
@@ -206,15 +217,17 @@
 
     def relay(piece):
         remote["y", piece].wait_recv()
-        axis, who = halves(piece), rank_of(piece)
-        if axis != "z":
+        axis, who = route(piece), rank_of(piece)
+        if axis in ("x", None):
             forward("x", piece, who, x_mate)
-        if axis != "x":
+        if axis in ("z", None):
             forward("z", piece, who, z_mate)
         forward("c0", piece, who, core_mate)
 
     def relay_again(piece):
-        axis = halves(piece)
+        axis = route(piece)
+        if axis == "y":
+            return
         if axis:
             remote[axis, piece].wait_recv()
             forward("c1", piece, mate_of(piece), core_mate)
@@ -230,7 +243,7 @@
         forward("c2", piece, z_rank, core_mate)
 
     def relay_last(piece):
-        if halves(piece):
+        if route(piece):
             return
         remote["g", piece].wait_recv()
         forward("c3", piece, g_rank, core_mate)
@@ -251,10 +264,11 @@
     def ready(kind, p):
         if done[2] < mark[kind, p]:
             top = -(-mark[kind, p] * 16 // len(order))
-            go(top, top, 0 if HALVES.get((kind, p)) else top)
+            axis = ROUTES.get((kind, p))
+            go(top, 0 if axis == "y" else top, 0 if axis else top)
         for piece in order:
             if (piece[0], piece[2]) == (kind, p):
-                for name in ("c0", "c1") if halves(piece) else ("c0", "c1", "c2", "c3"):
+                for name in ("c0", "c1", "c2", "c3")[:{"y": 1, None: 4}.get(route(piece), 2)]:
                     remote[name, piece].wait_recv()
 
     def lane(i, size):
@@ -374,10 +388,14 @@
     states(0, 0, heads, scan_a.state, 0)
     scan_a.begin()
     go(2, 0, 0)
+    if outer > 2:
+        learn(2)
     loads[3].wait()
     project_own(2)
     go(4, 0, 0)
     inner_next()
+    for k in range(3, outer):
+        learn(k)
     go(5, 2, 0)
     inner_next()
     scan_a.middle()
@@ -398,32 +416,33 @@
     ready(1, 0)
     project(1, 0)
     states_b(0)
-    go(14, 9, 4)
+    go(12, 9, 4)
     if pairs > 1:
         ready(1, final)
         project(1, final)
         states_b(final)
-    go(16, 10, 8)
+    go(13, 10, 8)
     scan_a.end()
+    loads[5].wait()
     finish(0, 0, heads, scan_a.prior, 0)
-    go(16, 12, 9)
+    go(13, 12, 9)
     scan_b[0].middle()
     loads[4].wait()
     join_own()
-    go(16, 13, 10)
+    go(14, 12, 10)
     if pairs > 1:
         scan_b[final].middle()
     ready(2, 0)
     project(2, 0)
     inner_b(0)
-    go(16, 15, 11)
+    go(14, 12, 11)
     scan_b[0].last()
     if pairs > 1:
         ready(2, final)
         project(2, final)
         inner_b(final)
         scan_b[final].last()
-    go(16, 16, 14)
+    go(14, 12, 12)
     finish_b(0)
     ready(3, 0)
     join(0)
@@ -465,7 +484,7 @@
     out = pl.pallas_call(
         functools.partial(kernel, n, seqs, parts),
         out_shape=jax.ShapeDtypeStruct((length, width), BF16),
-        in_specs=[any_spec] * 5 + [vmem],
+        in_specs=[any_spec] * 6,
         out_specs=vmem,
         scratch_shapes=[
             pltpu.VMEM((length, width), BF16),
@@ -478,7 +497,7 @@
             pltpu.VMEM((n, length, cols), BF16),
             pltpu.VMEM((length, width), F32),
         ]
-        + [pltpu.SemaphoreType.DMA((5,))]
+        + [pltpu.VMEM((norm_gain.size // DH, DH), F32), pltpu.SemaphoreType.DMA((6,)), pltpu.SemaphoreType.REGULAR]
         + [pltpu.SemaphoreType.DMA((8, 4, n - 1, pairs, parts))] * 2
         + scans,
         compiler_params=pltpu.CompilerParams(

time: 45.2 us -> 42.3 us (0.936)
  Pallas kernels: 42.6 us -> 39.9 us
    pallas_call x1, Pallas kernels: 42.6 us -> 39.9 us  [body(): pl.pallas_call(functools.partial(kernel, n, seqs, parts), out_shape=jax.S...]
where the time goes in v3:
time: 42.3 us; the launch traced here: 42.2 us
  Pallas kernels  39.9 us (94%)
  local copies, waits for them, and re-layouts  2.26 us (5%)
    pallas_call x1, Pallas kernels, body(): pl.pallas_call(functools.partial(kernel, n, seqs, parts), out_shape=jax.S...  39.9 us
    unnamed x1, local copies, waits for them, and re-layouts  2.26 us

profile of v3, /device:TPU:0, one launch (start us, length us, event | category | flops | bytes accessed | tf_op | source)
XLA Modules:
  0.0 42.2 jit_solution(13171278364317746907)
XLA Ops:
  0.0 39.9 %shard_map.64 = bf16[512,1024]{1,0:T(8,128)(2,1)} custom-call(bf16[512,1024]{1,0:T(8,128)(2,1)} %bitcast.4, bf16[1024,512]{1,0:T(8,128)(2,1)} %wq_hbm.1, bf16[1024,512]{1,0:T(8,128)(2,1)} %wk_hbm.1, bf16[1024,512]{1,0:T(8,128)(2,1)} %wv_hbm.1, bf16[512,1024]{1,0:T(8,128)(2,1)} %wo_hbm.1, f32[8,128]{1,0:T(8,128)} %bitcast.5), custom_call_target="tpu_custom_call" | custom-call | tf_op jit(solution)/shard_map/pallas_call | solution.py:484
  39.9 2.3 %copy.8 = bf16[1,512,1024]{2,1,0:T(8,128)(2,1)} copy(bf16[1,512,1024]{2,1,0:T(8,128)(2,1)} %bitcast.3) | data formatting | bytes 2097152

commit v4 on v3

--- a/solution.py
+++ b/solution.py
@@ -11,7 +11,7 @@
 GROUP = 8
 PLANE = 4
 LAG = 4
-ROUTES = {(0, 1): "x", (1, 1): "z", (3, 0): "y", (3, 1): "y"}
+ROUTES = {(0, 1, 0): "x", (0, 1, 1): "z", (1, 1, 0): "x", (1, 1, 1): "z", (2, 0, 0): "x", (2, 0, 1): "z", (2, 1, 0): "x", (2, 1, 1): "z", (3, 0, 0): "y", (3, 0, 1): "y", (3, 1, 0): "y", (3, 1, 1): "y"}
 MESH = pl.DeviceIdType.MESH
 F32 = jnp.float32
 BF16 = jnp.bfloat16
@@ -106,9 +106,9 @@
 
 def kernel(
     n, seqs, parts,
-    tok_hbm, wq_hbm, wk_hbm, wv_hbm, wo_hbm, gain_hbm, out_ref,
+    tok_hbm, wq_hbm, wk_hbm, wv_hbm, wo_hbm, gain_hbm, out_hbm,
     tok, own, own_o, wide, wide_o, kvq, within, normed, acc,
-    gain_ref, load_sem, enter, sends, recvs, *scan_refs,
+    gain_ref, out_ref, load_sem, enter, sends, recvs, *scan_refs,
 ):
     dp, seq = lax.axis_index("dp"), lax.axis_index("seq")
     length, width = tok.shape
@@ -158,7 +158,7 @@
         pl.when(row + k < outer)(lambda: pl.semaphore_wait(enter, 1))
 
     def route(piece):
-        return ROUTES.get((piece[0], piece[2]))
+        return ROUTES.get((piece[0], piece[2], piece[3]))
 
     def rank_of(piece):
         axis = route(piece)
@@ -264,8 +264,8 @@
     def ready(kind, p):
         if done[2] < mark[kind, p]:
             top = -(-mark[kind, p] * 16 // len(order))
-            axis = ROUTES.get((kind, p))
-            go(top, 0 if axis == "y" else top, 0 if axis else top)
+            used = {route(piece) for piece in order if (piece[0], piece[2]) == (kind, p)}
+            go(top, 0 if used == {"y"} else top, top if None in used else 0)
         for piece in order:
             if (piece[0], piece[2]) == (kind, p):
                 for name in ("c0", "c1", "c2", "c3")[:{"y": 1, None: 4}.get(route(piece), 2)]:
@@ -339,6 +339,10 @@
             at = lane(i, 256)
             acc[:, at] = jnp.dot(normed[0], own_o[:, at], preferred_element_type=F32)
 
+    def store(i):
+        at = lane(i, 256)
+        return pltpu.make_async_copy(out_ref.at[:, at], out_hbm.at[:, at], load_sem.at[6 + i])
+
     def join(p):
         for slot in range(1, n):
             @pl.loop(0, width // 256)
@@ -350,6 +354,7 @@
                 )
                 if slot == n - 1 and p == pairs - 1:
                     out_ref[:, at] = part.astype(BF16)
+                    store(i).start()
                 else:
                     acc[:, at] = part
 
@@ -407,29 +412,29 @@
     go(9, 5, 3)
     ready(0, 0)
     project(0, 0)
-    go(10, 6, 3)
+    go(9, 6, 3)
     scan_a.last()
-    go(12, 7, 4)
+    go(10, 7, 4)
     if pairs > 1:
         ready(0, final)
         project(0, final)
     ready(1, 0)
     project(1, 0)
     states_b(0)
-    go(12, 9, 4)
+    go(11, 8, 4)
     if pairs > 1:
         ready(1, final)
         project(1, final)
         states_b(final)
-    go(13, 10, 8)
+    go(12, 9, 8)
     scan_a.end()
     loads[5].wait()
     finish(0, 0, heads, scan_a.prior, 0)
-    go(13, 12, 9)
+    go(13, 10, 9)
     scan_b[0].middle()
     loads[4].wait()
     join_own()
-    go(14, 12, 10)
+    go(13, 11, 10)
     if pairs > 1:
         scan_b[final].middle()
     ready(2, 0)
@@ -453,6 +458,8 @@
         join(final)
     for copy in sent:
         copy.wait_send()
+    for i in range(width // 256):
+        store(i).wait()
     for scan in scans:
         scan.close()
 
@@ -466,7 +473,6 @@
     parts = 2 if n <= 2 else 1
     outer = seqs // PLANE
     any_spec = pl.BlockSpec(memory_space=pl.ANY)
-    vmem = pl.BlockSpec(memory_space=pltpu.VMEM)
     scans = []
     for rows in [cols] + [(n - 1) * lanes_per] * pairs:
         share = rows // PLANE
@@ -485,7 +491,7 @@
         functools.partial(kernel, n, seqs, parts),
         out_shape=jax.ShapeDtypeStruct((length, width), BF16),
         in_specs=[any_spec] * 6,
-        out_specs=vmem,
+        out_specs=any_spec,
         scratch_shapes=[
             pltpu.VMEM((length, width), BF16),
             pltpu.VMEM((3, width, cols), BF16),
@@ -497,7 +503,7 @@
             pltpu.VMEM((n, length, cols), BF16),
             pltpu.VMEM((length, width), F32),
         ]
-        + [pltpu.VMEM((norm_gain.size // DH, DH), F32), pltpu.SemaphoreType.DMA((6,)), pltpu.SemaphoreType.REGULAR]
+        + [pltpu.VMEM((norm_gain.size // DH, DH), F32), pltpu.VMEM((length, width), BF16), pltpu.SemaphoreType.DMA((6 + width // 256,)), pltpu.SemaphoreType.REGULAR]
         + [pltpu.SemaphoreType.DMA((8, 4, n - 1, pairs, parts))] * 2
         + scans,
         compiler_params=pltpu.CompilerParams(

time: 42.3 us -> 40.1 us (0.948)
  Pallas kernels: 39.9 us -> 37.7 us
    pallas_call x1, Pallas kernels: 39.9 us -> 37.7 us  [body(): pl.pallas_call(functools.partial(kernel, n, seqs, parts), out_shape=jax.S...]
where the time goes in v4:
time: 40.1 us; the launch traced here: 40 us
  Pallas kernels  37.7 us (94%)
  local copies, waits for them, and re-layouts  2.26 us (6%)
    pallas_call x1, Pallas kernels, body(): pl.pallas_call(functools.partial(kernel, n, seqs, parts), out_shape=jax.S...  37.7 us
    unnamed x1, local copies, waits for them, and re-layouts  2.26 us

profile of v4, /device:TPU:0, one launch (start us, length us, event | category | flops | bytes accessed | tf_op | source)
XLA Modules:
  0.0 40.0 jit_solution(6007707123551440085)
XLA Ops:
  0.0 37.7 %shard_map.64 = bf16[512,1024]{1,0:T(8,128)(2,1)} custom-call(bf16[512,1024]{1,0:T(8,128)(2,1)} %bitcast.4, bf16[1024,512]{1,0:T(8,128)(2,1)} %wq_hbm.1, bf16[1024,512]{1,0:T(8,128)(2,1)} %wk_hbm.1, bf16[1024,512]{1,0:T(8,128)(2,1)} %wv_hbm.1, bf16[512,1024]{1,0:T(8,128)(2,1)} %wo_hbm.1, f32[8,128]{1,0:T(8,128)} %bitcast.5), custom_call_target="tpu_custom_call" | custom-call | tf_op jit(solution)/shard_map/pallas_call | solution.py:490
  37.7 2.3 %copy.8 = bf16[1,512,1024]{2,1,0:T(8,128)(2,1)} copy(bf16[1,512,1024]{2,1,0:T(8,128)(2,1)} %bitcast.3) | data formatting | bytes 2097152
